TPU v7x, 256 devices: a whole 4x4x8 slice. The times are simulated.
256 devices in a mesh: dp: 4 (over y), fsdp: 8 (over z), tensor: 8 (over x, core).
Axes of the slice: x: 4, y: 4, z: 8, core: 2. Of those that a mesh axis runs over, the one named last changes fastest.
Arguments:
- momentum: bfloat16 [4, 8192, 8192], P('dp', 'fsdp', 'tensor'), may hold values from -24 to 24
- gradient: bfloat16 [4, 8192, 8192], P('dp', 'fsdp', 'tensor'), may hold values from -4 to 4
- factor: float32 [8192, 256], P('tensor'), may hold values from -6 to 6
Outputs:
- new_momentum: float32 [4, 8192, 8192], P('dp', 'fsdp', 'tensor')
- step_direction: bfloat16 [8192, 8192], P('fsdp', 'tensor')
- new_factor: float32 [8192, 256], P('tensor')
All inputs are finite; a program needn't handle non-finite values.
Results may differ from a plain program's by a relative error of at most 0.0065.
Values may be sent and summed in bfloat16 or wider, within the bound.
A program may use at most 64 MiB of HBM per device.

v0:
```python
import jax
import jax.numpy as jnp
from jax import lax
from jax.sharding import PartitionSpec as P

ROWS = 8192
COLS = 8192
RANK = 256


def orthonormal(rows_part, gram):
    lower = jnp.linalg.cholesky(gram)
    return jax.scipy.linalg.solve_triangular(lower, rows_part.T, lower=True).T


def transposed_product(block, ortho_low):
    return lax.dot_general(
        block, ortho_low, (((0,), (0,)), ((), ())), preferred_element_type=jnp.float32
    )


def local(momentum, gradient, factor):
    highest = lax.Precision.HIGHEST
    replicas = lax.axis_size("dp")
    moment = momentum[0]
    change = gradient[0]
    factor_low = factor.astype(jnp.bfloat16)
    partial_left = jnp.dot(moment, factor_low, preferred_element_type=jnp.float32)
    partial_left = partial_left + jnp.dot(change, factor_low, preferred_element_type=jnp.float32)
    left = lax.psum(partial_left, ("dp", "tensor")) / replicas
    gram = lax.psum(jnp.dot(left.T, left, precision=highest), "fsdp")
    ortho_low = orthonormal(left, gram).astype(jnp.bfloat16)
    partial_right = transposed_product(moment, ortho_low) + transposed_product(change, ortho_low)
    right = lax.psum(partial_right, ("dp", "fsdp")) / replicas
    square_sums = lax.psum(jnp.sum(right * right, axis=0), "tensor")
    new_factor = right / jnp.sqrt(square_sums / COLS + 1e-06)
    right_low = right.astype(jnp.bfloat16)
    feedback = jnp.dot(ortho_low, right_low.T, preferred_element_type=jnp.float32)
    new_momentum = (moment.astype(jnp.float32) + change.astype(jnp.float32) - 0.05 * feedback)[None]
    step_scale = jnp.sqrt(jnp.float32(ROWS / RANK))
    factor_next_low = new_factor.astype(jnp.bfloat16)
    step_direction = (
        step_scale * jnp.dot(ortho_low, factor_next_low.T, preferred_element_type=jnp.float32)
    ).astype(jnp.bfloat16)
    return (new_momentum, step_direction, new_factor)


def solution(mesh):
    in_specs = (P("dp", "fsdp", "tensor"), P("dp", "fsdp", "tensor"), P("tensor", None))
    out_specs = (P("dp", "fsdp", "tensor"), P("fsdp", "tensor"), P("tensor", None))
    return jax.shard_map(local, mesh=mesh, in_specs=in_specs, out_specs=out_specs, check_vma=False)
```

profile of v0, /device:TPU:1, one launch (start us, length us, event | category | flops | bytes accessed | tf_op | source)
XLA Modules:
  0.0 455.1 jit_solution(12589717732364756060)
XLA Ops:
  7.2 0.0 copy-start.1
  7.2 0.0 all-reduce.5.cloned.1.call-start
  7.2 2.7 fusion.2
  10.0 0.0 copy-done.7
  10.0 0.1 copy-done.1
  10.0 1.7 fusion.8
  11.7 0.0 all-reduce.5.cloned.1.call-update
  11.7 0.0 all-reduce.7.cloned.1.call-start
  11.8 119.2 %all-reduce.5.cloned.1.call-done = f32[1024,256]{1,0:T(8,128)} async-done(((f32[1024,256]{1,0:T(8,128)}), f32[1024,256]{1,0:T(8,128)}) %all-reduce.5.cloned.1.call-update) | async-done | bytes 1048592 | tf_op jit(solution)/shard_map/psum | solution.py:30
  131.0 4.2 fusion.17
  135.2 0.0 all-reduce.7.cloned.1.call-update
  135.2 0.2 all-reduce.9.cloned.1.call-start
  135.5 0.1 multiply_bitcast_fusion
  135.5 67.4 %all-reduce.7.cloned.1.call-done = f32[256,256]{0,1:T(8,128)} async-done(((f32[256,256]{0,1:T(8,128)}), f32[256,256]{0,1:T(8,128)}) %all-reduce.7.cloned.1.call-update) | async-done | bytes 262160 | tf_op jit(solution)/shard_map/psum | solution.py:31
  203.0 1.1 copy.7
  204.1 1.0 fusion.24
  205.1 11.7 %cholesky.50 = f32[128,128]{1,0:T(8,128)S(1)} custom-call(f32[128,128]{1,0:T(8,128)S(1)} %cholesky.118), custom_call_target="Cholesky" | custom-call | tf_op jit(solution)/shard_map/jit(cholesky)/cholesky | solution.py:12
  216.8 9.8 %custom-call.15 = f32[1,128,128]{1,2,0:T(8,128)S(1)} custom-call(f32[1,128,128]{2,1,0:T(8,128)S(1)} %get-tuple-element.24), custom_call_target="InvertDiagBlocksLowerTriangular" | custom-call | tf_op jit(solution)/shard_map/jit(cholesky)/cholesky | solution.py:12
  226.7 0.2 constant_dynamic-update-slice_fusion.1
  226.9 0.3 convolution_subtract_fusion.1
  227.1 11.7 %cholesky.105 = f32[128,128]{1,0:T(8,128)S(1)} custom-call(f32[128,128]{1,0:T(8,128)S(1)} %convolution_subtract_fusion.1), custom_call_target="Cholesky" | custom-call | tf_op jit(solution)/shard_map/jit(cholesky)/cholesky | solution.py:12
  238.9 0.6 compare_reduce_fusion
  240.8 0.7 select_select_fusion
  241.6 0.1 triangular_solve.57
  241.6 5.8 %while.1 = (s32[]{:T(128)}, f32[256,256]{1,0:T(8,128)}, s32[2,2]{1,0:T(2,128)S(1)}, f32[2,128,128]{2,1,0:T(8,128)S(1)}, s32[]{:T(128)}) while((s32[]{:T(128)}, f32[256,256]{1,0:T(8,128)}, s32[2,2]{1,0:T(2,128)S(1)}, f32[2,128,128]{2,1,0:T(8,128)S(1)}, s32[]{:T(128)}) %tuple.28), condition=%wide.while_cond, body=%wide.while_body.sunk | while | flops 2 | bytes 131189 | solution.py:13
  241.6 0.6 fusion.40
  242.2 2.3 bitcast_dynamic-update-slice_fusion.2
  244.6 0.6 fusion.40
  245.2 2.3 bitcast_dynamic-update-slice_fusion.2
  247.5 0.0 copy-start
  247.5 19.7 %custom-call.16 = f32[2,128,128]{1,2,0:T(8,128)S(1)} custom-call(f32[2,128,128]{2,1,0:T(8,128)S(1)} %get-tuple-element.10), custom_call_target="InvertDiagBlocksLowerTriangular" | custom-call | tf_op jit(solution)/shard_map/jit(_solve_triangular)/triangular_solve | solution.py:13
  267.2 0.6 fusion.34
  267.8 1.8 convolution_subtract_fusion
  269.7 0.0 copy-start.2
  269.7 0.6 convolution_convert_fusion
  270.3 0.9 fusion
  271.3 1.9 fusion.14
  273.2 0.0 all-reduce.9.cloned.1.call-update
  273.3 149.4 %all-reduce.9.cloned.1.call-done = f32[1024,256]{1,0:T(8,128)} async-done(((f32[1024,256]{1,0:T(8,128)}), f32[1024,256]{1,0:T(8,128)}) %all-reduce.9.cloned.1.call-update) | async-done | bytes 1048592 | tf_op jit(solution)/shard_map/psum | solution.py:34
  422.6 1.4 multiply_reduce_fusion
  424.0 17.3 %psum.31 = f32[256]{0:T(256)S(1)} all-reduce(f32[256]{0:T(256)S(1)} %multiply_reduce_fusion), channel_id=1, replica_groups=mesh['dp'=4,'fsdp'=8,'tensor'=8] {'tensor'}, use_global_device_ids=true, to_apply=%region_8.9 | all-reduce | flops 256 | bytes 2048 | tf_op jit(solution)/shard_map/psum | solution.py:35
  441.3 1.3 multiply_divide_fusion
  442.6 0.0 copy-start.6
  442.6 0.0 copy-start.3
  442.7 2.1 multiply_convert_fusion
  444.8 0.3 copy-done.3
  445.0 0.6 copy-done.4
  445.6 2.9 subtract_bitcast_fusion
  (16 shorter events, 0.1 us)
Async XLA Ops:
  7.2 2.8 copy-start.7
  7.2 2.9 copy-start.1
  7.2 123.8 %all-reduce.5.cloned.1.call-start = ((), (), s32[]{:S(2)}) async-start(), calls=%async_computation | async-start | bytes 2097152 | tf_op jit(solution)/shard_map/psum | solution.py:30
  11.7 191.2 %all-reduce.7.cloned.1.call-start = ((), (), s32[]{:S(2)}) async-start(), calls=%async_computation.1 | async-start | bytes 524288 | tf_op jit(solution)/shard_map/psum | solution.py:31
  131.0 4.4 copy-start.5
  135.2 287.4 %all-reduce.9.cloned.1.call-start = ((), (), s32[]{:S(2)}) async-start(), calls=%async_computation.2 | async-start | bytes 2097152 | tf_op jit(solution)/shard_map/psum | solution.py:34
  247.5 22.9 %copy-start = (bf16[1,1024,1024]{2,1,0:T(8,128)(2,1)S(1)}, bf16[1,1024,1024]{2,1,0:T(8,128)(2,1)}, u32[]{:S(2)}) copy-start(bf16[1,1024,1024]{2,1,0:T(8,128)(2,1)} %param.4) | copy-start | bytes 6291460
  269.7 1.6 copy-start.2
  442.6 6.0 %copy-start.6 = (f32[1024,256]{1,0:T(8,128)}, f32[1024,256]{1,0:T(8,128)S(1)}, u32[]{:S(2)}) copy-start(f32[1024,256]{1,0:T(8,128)S(1)} %multiply_divide_fusion) | copy-start | bytes 3145732
  442.6 2.4 copy-start.3
  442.7 3.0 copy-start.4
Sparse Core Ops, SparseCore 0:
  11.9 119.1 all-reduce.4
  135.3 67.5 all-reduce.6
  273.4 149.1 all-reduce.8
where the time goes:
time: 456 us; the launch traced here: 455 us
  waiting for transfers between devices  336 us (74%)
  other arithmetic  58.1 us (13%)
  matrix products  20.1 us (4%)
  blocking collectives  17.3 us (4%)
  between operations  15.3 us (3%)
  local copies, waits for them, and re-layouts  7.94 us (2%)
    psum x1, waiting for transfers between devices, local(): right = lax.psum(partial_right, ('dp', 'fsdp')) / replicas  149 us
    psum x1, waiting for transfers between devices, local(): left = lax.psum(partial_left, ('dp', 'tensor')) / replicas  119 us
    psum x1, waiting for transfers between devices, local(): gram = lax.psum(jnp.dot(left.T, left, precision=highest), 'fsdp')  67.4 us
    another operation x6, other arithmetic, orthonormal(): lower = jnp.linalg.cholesky(gram)  33.9 us
    another operation x3, other arithmetic, orthonormal(): return jax.scipy.linalg.solve_triangular(lower, rows_part.T, lower=True).T  20.4 us
    psum x1, blocking collectives, local(): square_sums = lax.psum(jnp.sum(right * right, axis=0), 'tensor')  17.3 us
  transfers between devices with their start and end apart: 3, of which 3 were waited for; matrix products, arithmetic and copies ran while one was open for 0% of the time, Pallas kernels for 0%

commit v1 on v0

v1 whole, which is shorter than its diff:
```python
import jax
import jax.numpy as jnp
from jax import lax
from jax.experimental import pallas as pl
from jax.experimental.pallas import tpu as pltpu
from jax.sharding import PartitionSpec as P

ROWS = 8192
COLS = 8192
RANK = 256

MESH = pl.DeviceIdType.MESH
HIGHEST = lax.Precision.HIGHEST
F32 = jnp.float32
BF16 = jnp.bfloat16
BLOCK = 64
BLOCKS = RANK // BLOCK
Y, Z, X = 4, 8, 4
CHIPS = X * Y
PLANE = Y * Z
LOCAL = 1024
HALF = LOCAL // 2
OWN = LOCAL // (2 * CHIPS)
PARTS = 8
CHUNK = LOCAL // PARTS
QUARTER = LOCAL // Y


def dot(a, b):
    return jnp.dot(a, b, precision=HIGHEST, preferred_element_type=F32)


def low_dot(a, b):
    return jnp.dot(a, b, preferred_element_type=F32)


def factor_block(w, size):
    lanes = w.shape[1]
    row = lax.broadcasted_iota(jnp.int32, (8, lanes), 0)
    done = []
    for j in range(0, size, 8):
        v = w[0:8, :]
        p = [jnp.broadcast_to(v[m : m + 1, :], (8, lanes)) for m in range(8)]
        a = [
            [jnp.broadcast_to(p[i][:, j + m : j + m + 1], (8, lanes)) for m in range(i + 1)]
            for i in range(8)
        ]
        rest = w[8:, :]
        n = rest.shape[0]
        columns = [jnp.broadcast_to(rest[:, j + m : j + m + 1], (n, lanes)) for m in range(8)] if n else []
        low = [[None] * 8 for _ in range(8)]
        inverse = [None] * 8
        for k in range(8):
            inverse[k] = 1.0 / a[k][k]
            for i in range(k + 1, 8):
                low[i][k] = a[i][k] * inverse[k]
            for i in range(k + 1, 8):
                for m in range(k + 1, i + 1):
                    a[i][m] = a[i][m] - low[i][k] * a[m][k]
            for i in range(k + 1, 8):
                p[i] = p[i] - low[i][k] * p[k]
        out = p[7] * lax.rsqrt(a[7][7])
        for k in range(6, -1, -1):
            out = jnp.where(row == k, p[k] * lax.rsqrt(a[k][k]), out)
        done.append(out)
        if n:
            q = [None] * 8
            for k in range(7, -1, -1):
                q[k] = p[k] * inverse[k]
                for i in range(7, k, -1):
                    q[k] = q[k] - low[i][k] * q[i]
            for k in range(8):
                rest = rest - columns[k] * jnp.broadcast_to(q[k][0:1, :], (n, lanes))
            w = rest
    return jnp.concatenate(done, axis=0)


def eliminate(gram, inv, block):
    lo, hi = block * BLOCK, (block + 1) * BLOCK
    rows = gram[lo:hi, :]
    r_i = lax.broadcasted_iota(jnp.int32, (BLOCK, BLOCK), 0)
    c_i = lax.broadcasted_iota(jnp.int32, (BLOCK, BLOCK), 1)
    eye = jnp.where(r_i == c_i, 1.0, 0.0).astype(F32)
    root = factor_block(jnp.concatenate([rows[:, lo:hi], eye], axis=1), BLOCK)[:, BLOCK:]
    mine = dot(root, inv[lo:hi, :])
    inv[lo:hi, :] = mine
    if hi < RANK:
        upper = dot(root, rows)
        below = upper.T[hi:, :]
        gram[hi:, :] = gram[hi:, :] - dot(below, upper)
        inv[hi:, :] = inv[hi:, :] - dot(below, mine)
    return mine


def remote(src, dst, send, recv, **where):
    return pltpu.make_async_remote_copy(
        src_ref=src, dst_ref=dst, send_sem=send, recv_sem=recv, device_id=where, device_id_type=MESH
    )


def take(ref, sem):
    pltpu.make_async_copy(ref, ref, sem).wait()


def core_kernel(
    m_hbm, g_hbm, f_ref,
    ortho_t, right_t, squares,
    mv, gv, fv, part, partner_in, half, outgoing, incoming, left, left_t,
    gram, gram_in, gram_all, work, inv, rs_out, rs_in, spread, square_in,
    load_sem, pair_sem, rs_sem, ag_send, ag_recv, fw_send, fw_recv,
    z_sem, gg_send, gg_recv, gf_send, gf_recv, r_send, r_recv, s_send, s_recv, n_sem,
):
    y = lax.axis_index("dp")
    z = lax.axis_index("fsdp")
    t = lax.axis_index("tensor")
    x = t // 2
    c = lax.rem(t, 2)
    other = t + 1 - 2 * c
    chip = y * X + x
    me = c * CHIPS + chip

    def first_row(i):
        half_of = jnp.where(i < PARTS // 2, 1 - c, c)
        return pl.multiple_of(half_of * HALF + lax.rem(i, PARTS // 2) * CHUNK, CHUNK)

    def load(i, which):
        src, dst = ((m_hbm, mv), (g_hbm, gv))[which]
        rows = pl.ds(first_row(i), CHUNK)
        return pltpu.make_async_copy(src.at[rows, :], dst.at[rows, :], load_sem.at[which, i])

    for i in range(PARTS):
        load(i, 0).start()
        load(i, 1).start()

    def chip_at(d):
        return lax.rem(y + d // X, Y), lax.rem(x + lax.rem(d, X), X)

    def line_at(d):
        return lax.rem(y + d // Z, Y), lax.rem(z + lax.rem(d, Z), Z)

    barrier = pltpu.get_barrier_semaphore()

    @pl.loop(1, CHIPS)
    def _(d):
        py, px = chip_at(d)
        pl.semaphore_signal(barrier, inc=1, device_id={"dp": py, "fsdp": z, "tensor": px * 2 + c}, device_id_type=MESH)

    @pl.loop(1, PLANE)
    def _(d):
        py, pz = line_at(d)
        pl.semaphore_signal(barrier, inc=1, device_id={"dp": py, "fsdp": pz, "tensor": t}, device_id_type=MESH)

    @pl.loop(1, 2 * X)
    def _(d):
        pl.semaphore_signal(barrier, inc=1, device_id={"dp": y, "fsdp": z, "tensor": lax.rem(t + d, 2 * X)}, device_id_type=MESH)

    fv[...] = f_ref[...].astype(BF16)

    def product(i):
        load(i, 0).wait()
        load(i, 1).wait()
        rows = pl.ds(first_row(i), CHUNK)
        part[pl.ds(pl.multiple_of(i * CHUNK, CHUNK), CHUNK), :] = low_dot(mv[rows, :], fv[...]) + low_dot(gv[rows, :], fv[...])

    @pl.loop(0, PARTS // 2)
    def _(i):
        product(i)

    pl.semaphore_wait(barrier, CHIPS - 1 + PLANE - 1 + 2 * X - 1)
    to_partner = remote(part.at[0:HALF, :], partner_in, pair_sem.at[0], pair_sem.at[1], dp=y, fsdp=z, tensor=other)
    to_partner.start()

    @pl.loop(PARTS // 2, PARTS)
    def _(i):
        product(i)

    to_partner.wait_recv()
    total = (part[HALF:, :] + partner_in[...]).reshape(CHIPS, OWN, RANK)
    half[...] = total
    outgoing[...] = total.astype(BF16)

    @pl.loop(1, CHIPS)
    def _(d):
        py, px = chip_at(d)
        remote(outgoing.at[py * X + px], incoming.at[d], rs_sem.at[0], rs_sem.at[1], dp=py, fsdp=z, tensor=px * 2 + c).start()

    take(incoming.at[1:], rs_sem.at[1])
    mine = half[chip]
    for d in range(1, CHIPS):
        mine = mine + incoming[d].astype(F32)
    left[me] = mine * 0.25

    def left_copy(d):
        py, px = chip_at(d)
        return remote(left.at[me], left.at[me], ag_send.at[d], ag_recv.at[d], dp=py, fsdp=z, tensor=px * 2 + c)

    def left_forward(d):
        py, px = lax.rem(y + Y - d // X, Y), lax.rem(x + X - lax.rem(d, X), X)
        slot = c * CHIPS + py * X + px
        return remote(left.at[slot], left.at[slot], fw_send.at[d], fw_recv.at[d], dp=y, fsdp=z, tensor=other)

    @pl.loop(1, CHIPS)
    def _(d):
        left_copy(d).start()

    left_forward(0).start()

    @pl.loop(1, CHIPS)
    def _(d):
        left_copy(d).wait_recv()
        left_forward(d).start()

    @pl.loop(0, CHIPS)
    def _(d):
        left_forward(d).wait_recv()

    rows = left[...].reshape(LOCAL, RANK)
    left_t[...] = rows.T
    gram[...] = dot(left_t[...], rows).reshape(2 * CHIPS, 8, RANK)

    @pl.loop(1, Z)
    def _(d):
        remote(gram.at[me], gram_in.at[d], z_sem.at[0], z_sem.at[1], dp=y, fsdp=lax.rem(z + d, Z), tensor=t).start()

    take(gram_in.at[1:], z_sem.at[1])
    mine = gram[me]
    for d in range(1, Z):
        mine = mine + gram_in[d]
    gram_all[me] = mine

    def gram_copy(d):
        py, px = chip_at(d)
        return remote(gram_all.at[me], gram_all.at[me], gg_send.at[d], gg_recv.at[d], dp=py, fsdp=z, tensor=px * 2 + c)

    def gram_forward(d):
        py, px = lax.rem(y + Y - d // X, Y), lax.rem(x + X - lax.rem(d, X), X)
        slot = c * CHIPS + py * X + px
        return remote(gram_all.at[slot], gram_all.at[slot], gf_send.at[d], gf_recv.at[d], dp=y, fsdp=z, tensor=other)

    @pl.loop(1, CHIPS)
    def _(d):
        gram_copy(d).start()

    gram_forward(0).start()

    @pl.loop(1, CHIPS)
    def _(d):
        gram_copy(d).wait_recv()
        gram_forward(d).start()

    @pl.loop(0, CHIPS)
    def _(d):
        gram_forward(d).wait_recv()

    work[...] = gram_all[...].reshape(RANK, RANK)
    r_i = lax.broadcasted_iota(jnp.int32, (RANK, RANK), 0)
    c_i = lax.broadcasted_iota(jnp.int32, (RANK, RANK), 1)
    inv[...] = jnp.where(r_i == c_i, 1.0, 0.0).astype(F32)

    def right_send(b):
        @pl.loop(1, PLANE)
        def _(d):
            py, pz = line_at(d)
            remote(rs_out.at[b, py * Z + pz], rs_in.at[b, d], r_send.at[b], r_recv.at[b], dp=py, fsdp=pz, tensor=t).start()

    def right_sum(b):
        take(rs_in.at[b, 1:], r_recv.at[b])
        mine = rs_out[b, y * Z + z].astype(F32)
        for d in range(1, PLANE):
            mine = mine + rs_in[b, d].astype(F32)
        spread[b, y * Z + z] = (mine * 0.25).astype(BF16)

        @pl.loop(1, PLANE)
        def _(d):
            py, pz = line_at(d)
            slot = spread.at[b, y * Z + z]
            remote(slot, slot, s_send.at[b], s_recv.at[b], dp=py, fsdp=pz, tensor=t).start()

    for b in range(BLOCKS):
        rows_of = eliminate(work, inv, b)
        low = dot(rows_of, left_t[...]).astype(BF16)
        ortho_t[b * BLOCK : (b + 1) * BLOCK, :] = low
        term = low_dot(low, mv[...]) + low_dot(low, gv[...])
        for pz in range(Z):
            for py in range(Y):
                rs_out[b, py * Z + pz] = term[pz * 8 : pz * 8 + 8, py * QUARTER : (py + 1) * QUARTER].astype(BF16)
        right_send(b)
        if b:
            right_sum(b - 1)
    right_sum(BLOCKS - 1)

    sums = jnp.zeros((8, RANK), F32)
    for b in range(BLOCKS):
        take(spread.at[b, 1:], s_recv.at[b])
        for py in range(Y):
            for pz in range(0, Z, 2):
                two = jnp.concatenate([spread[b, py * Z + pz], spread[b, py * Z + pz + 1]], axis=0)
                right_t[b * BLOCK + pz * 8 : b * BLOCK + pz * 8 + 16, py * QUARTER : (py + 1) * QUARTER] = two
    full = right_t[...].astype(F32)
    ones = jnp.ones((8, LOCAL), F32)
    square_in[t] = lax.dot_general(ones, full * full, (((1,), (1,)), ((), ())), precision=HIGHEST, preferred_element_type=F32)

    @pl.loop(1, 2 * X)
    def _(d):
        remote(square_in.at[t], square_in.at[t], n_sem.at[0], n_sem.at[1], dp=y, fsdp=z, tensor=lax.rem(t + d, 2 * X)).start()

    take(square_in.at[1:], n_sem.at[1])
    sums = square_in[0]
    for d in range(1, 2 * X):
        sums = sums + square_in[d]
    squares[...] = sums

    to_partner.wait_send()
    take(outgoing.at[1:], rs_sem.at[0])

    @pl.loop(1, CHIPS)
    def _(d):
        left_copy(d).wait_send()
        gram_copy(d).wait_send()

    @pl.loop(0, CHIPS)
    def _(d):
        left_forward(d).wait_send()
        gram_forward(d).wait_send()

    take(gram_in.at[1:], z_sem.at[0])
    for b in range(BLOCKS):
        take(rs_out.at[b, 1:], r_send.at[b])
        take(spread.at[b, 1:], s_send.at[b])
    take(square_in.at[1:], n_sem.at[0])


def core(moment, change, factor):
    vmem = pl.BlockSpec(memory_space=pltpu.VMEM)
    hbm = pl.BlockSpec(memory_space=pl.ANY)
    dma = pltpu.SemaphoreType.DMA
    return pl.pallas_call(
        core_kernel,
        out_shape=(
            jax.ShapeDtypeStruct((RANK, LOCAL), BF16),
            jax.ShapeDtypeStruct((RANK, LOCAL), BF16),
            jax.ShapeDtypeStruct((8, RANK), F32),
        ),
        in_specs=[hbm, hbm, vmem],
        out_specs=(vmem, vmem, vmem),
        scratch_shapes=[
            pltpu.VMEM((LOCAL, LOCAL), BF16),
            pltpu.VMEM((LOCAL, LOCAL), BF16),
            pltpu.VMEM((LOCAL, RANK), BF16),
            pltpu.VMEM((LOCAL, RANK), F32),
            pltpu.VMEM((HALF, RANK), F32),
            pltpu.VMEM((CHIPS, OWN, RANK), F32),
            pltpu.VMEM((CHIPS, OWN, RANK), BF16),
            pltpu.VMEM((CHIPS, OWN, RANK), BF16),
            pltpu.VMEM((2 * CHIPS, OWN, RANK), F32),
            pltpu.VMEM((RANK, LOCAL), F32),
            pltpu.VMEM((2 * CHIPS, 8, RANK), F32),
            pltpu.VMEM((Z, 8, RANK), F32),
            pltpu.VMEM((2 * CHIPS, 8, RANK), F32),
            pltpu.VMEM((RANK, RANK), F32),
            pltpu.VMEM((RANK, RANK), F32),
            pltpu.VMEM((BLOCKS, PLANE, 8, QUARTER), BF16),
            pltpu.VMEM((BLOCKS, PLANE, 8, QUARTER), BF16),
            pltpu.VMEM((BLOCKS, PLANE, 8, QUARTER), BF16),
            pltpu.VMEM((2 * X, 8, RANK), F32),
            dma((2, PARTS)),
            dma((2,)),
            dma((2,)),
            dma((CHIPS,)),
            dma((CHIPS,)),
            dma((CHIPS,)),
            dma((CHIPS,)),
            dma((2,)),
            dma((CHIPS,)),
            dma((CHIPS,)),
            dma((CHIPS,)),
            dma((CHIPS,)),
            dma((BLOCKS,)),
            dma((BLOCKS,)),
            dma((BLOCKS,)),
            dma((BLOCKS,)),
            dma((2,)),
        ],
        compiler_params=pltpu.CompilerParams(
            collective_id=0, has_side_effects=True, vmem_limit_bytes=48 * 1024 * 1024
        ),
    )(moment, change, factor)


def final_kernel(m_ref, g_ref, o_ref, r_ref, r_part, s_ref, nm_ref, sd_ref, nf_ref, fv, iv):
    @pl.when(pl.program_id(0) == 0)
    def _():
        scale = lax.rsqrt(s_ref[...] * (1.0 / COLS) + 1e-06)
        iv[...] = jnp.broadcast_to(scale.T[:, 0:1], (RANK, 128))
        fv[...] = (r_ref[...].astype(F32) * iv[:, 0:1]).astype(BF16)

    across = (((0,), (0,)), ((), ()))
    ortho = o_ref[...].astype(F32).T.astype(BF16)
    feedback = low_dot(ortho, r_ref[...])
    nm_ref[...] = m_ref[...].astype(F32) + g_ref[...].astype(F32) - 0.05 * feedback
    sd_ref[...] = (jnp.sqrt(F32(ROWS / RANK)) * low_dot(ortho, fv[...])).astype(BF16)
    nf_ref[...] = (r_part[...].astype(F32) * iv[...]).T


def final(moment, change, ortho_t, right_t, squares):
    step = 128
    row = lambda i: (i, 0)
    col = lambda i: (0, i)
    fixed = lambda i: (0, 0)
    return pl.pallas_call(
        final_kernel,
        grid=(LOCAL // step,),
        out_shape=(
            jax.ShapeDtypeStruct((LOCAL, LOCAL), F32),
            jax.ShapeDtypeStruct((LOCAL, LOCAL), BF16),
            jax.ShapeDtypeStruct((LOCAL, RANK), F32),
        ),
        in_specs=[
            pl.BlockSpec((step, LOCAL), row),
            pl.BlockSpec((step, LOCAL), row),
            pl.BlockSpec((RANK, step), col),
            pl.BlockSpec((RANK, LOCAL), fixed),
            pl.BlockSpec((RANK, step), col),
            pl.BlockSpec((8, RANK), fixed),
        ],
        out_specs=(
            pl.BlockSpec((step, LOCAL), row),
            pl.BlockSpec((step, LOCAL), row),
            pl.BlockSpec((step, RANK), row),
        ),
        scratch_shapes=[pltpu.VMEM((RANK, LOCAL), BF16), pltpu.VMEM((RANK, 128), F32)],
    )(moment, change, ortho_t, right_t, right_t, squares)


def local(momentum, gradient, factor):
    ortho_t, right_t, squares = core(momentum[0], gradient[0], factor)
    new_momentum, step_direction, new_factor = final(momentum[0], gradient[0], ortho_t, right_t, squares)
    return new_momentum[None], step_direction, new_factor


def solution(mesh):
    in_specs = (P("dp", "fsdp", "tensor"), P("dp", "fsdp", "tensor"), P("tensor", None))
    out_specs = (P("dp", "fsdp", "tensor"), P("fsdp", "tensor"), P("tensor", None))
    return jax.shard_map(local, mesh=mesh, in_specs=in_specs, out_specs=out_specs, check_vma=False)
```

time: 456 us -> 103 us (0.23)
  waiting for transfers between devices: 336 us -> 0 us
  Pallas kernels: 0 us -> 96.8 us
  other arithmetic: 58.1 us -> 0 us
  matrix products: 20.1 us -> 0 us
  blocking collectives: 17.3 us -> 0 us
  between operations: 15.3 us -> 0.66 us
    psum x3 -> x0, waiting for transfers between devices: 336 us -> none  [the longest x1 149 us: local(): right = lax.psum(partial_right, ('dp', 'fsdp')) / replicas]
    pallas_call x0 -> x2, Pallas kernels: none -> 96.8 us  [the longest x1 87.6 us: core(): pl.pallas_call(core_kernel, out_shape=(jax.ShapeDtypeStruct((RANK, LOCAL)...]
    another operation x9 -> x0, other arithmetic: 54.4 us -> none  [the longest x6 33.9 us: orthonormal(): lower = jnp.linalg.cholesky(gram)]
    psum x1 -> x0, blocking collectives: 17.3 us -> none  [local(): square_sums = lax.psum(jnp.sum(right * right, axis=0), 'tensor')]
    dot_general x7 -> x0, matrix products: 16.5 us -> none  [the longest x1 4.17 us: local(): gram = lax.psum(jnp.dot(left.T, left, precision=highest), 'fsdp')]
    another operation x9 -> x0, local copies, waits for them, and re-layouts: 5.91 us -> none
  transfers between devices with their start and end apart: 3 -> 0, of which waited for: 3 -> 0; matrix products, arithmetic and copies ran while one was open for 0% -> 0% of each run, Pallas kernels for 0% -> 0%
where the time goes in v1:
time: 103 us; the launch traced here: 102 us
  Pallas kernels  96.8 us (94%)
  local copies, waits for them, and re-layouts  4.98 us (5%)
    pallas_call x1, Pallas kernels, core(): pl.pallas_call(core_kernel, out_shape=(jax.ShapeDtypeStruct((RANK, LOCAL)...  87.6 us
    pallas_call x1, Pallas kernels, final(): pl.pallas_call(final_kernel, grid=(LOCAL // step,), out_shape=(jax.ShapeD...  9.12 us
    unnamed x10, local copies, waits for them, and re-layouts  4.98 us

profile of v1, /device:TPU:1, one launch (start us, length us, event | category | flops | bytes accessed | tf_op | source)
XLA Modules:
  0.0 102.4 jit_solution(7929610198742732521)
XLA Ops:
  0.6 0.0 copy-start
  0.6 1.6 %copy-done = bf16[1,1024,1024]{2,1,0:T(8,128)(2,1)S(1)} copy-done((bf16[1,1024,1024]{2,1,0:T(8,128)(2,1)S(1)}, bf16[1,1024,1024]{2,1,0:T(8,128)(2,1)}, u32[]{:S(2)}) %copy-start) | copy-done | bytes 2097176
  2.2 0.0 copy-start.2
  2.2 1.2 %copy-done.2 = f32[1024,256]{1,0:T(8,128)S(1)} copy-done((f32[1024,256]{1,0:T(8,128)S(1)}, f32[1024,256]{1,0:T(8,128)}, u32[]{:S(2)}) %copy-start.2) | copy-done | bytes 1048600
  3.4 87.6 %shard_map.58 = (bf16[256,1024]{1,0:T(8,128)(2,1)S(1)}, bf16[256,1024]{1,0:T(8,128)(2,1)S(1)}, f32[8,256]{1,0:T(8,128)S(1)}) custom-call(bf16[1024,1024]{1,0:T(8,128)(2,1)S(1)} %bitcast.4, bf16[1024,1024]{1,0:T(8,128)(2,1)} %bitcast.5, f32[1024,256]{1,0:T(8,128)S(1)} %copy-done.2), custom_call_target="tpu_custom_call" | custom-call | tf_op jit(solution)/shard_map/pallas_call | solution.py:337
  91.1 0.0 copy-start.1
  91.1 0.8 copy-done.1
  91.9 0.0 copy-start.3
  91.9 0.8 copy-done.3
  92.7 0.0 copy-start.4
  92.7 0.6 copy-done.4
  93.3 9.1 %shard_map.59 = (f32[1024,1024]{1,0:T(8,128)}, bf16[1024,1024]{1,0:T(8,128)(2,1)}, f32[1024,256]{1,0:T(8,128)}) custom-call(bf16[1024,1024]{1,0:T(8,128)(2,1)} %bitcast.3, bf16[1024,1024]{1,0:T(8,128)(2,1)} %bitcast.6, bf16[256,1024]{1,0:T(8,128)(2,1)} %copy-done.3, bf16[256,1024]{1,0:T(8,128)(2,1)} %copy-done.1, bf16[256,1024]{1,0:T(8,128)(2,1)} %copy-done.1, ...), custom_call_target="tpu_custom_call" | custom-call | tf_op jit(solution)/shard_map/pallas_call | solution.py:410
Async XLA Ops:
  0.6 1.6 %copy-start = (bf16[1,1024,1024]{2,1,0:T(8,128)(2,1)S(1)}, bf16[1,1024,1024]{2,1,0:T(8,128)(2,1)}, u32[]{:S(2)}) copy-start(bf16[1,1024,1024]{2,1,0:T(8,128)(2,1)} %param.3) | copy-start | bytes 6291460
  2.2 1.2 %copy-start.2 = (f32[1024,256]{1,0:T(8,128)S(1)}, f32[1024,256]{1,0:T(8,128)}, u32[]{:S(2)}) copy-start(f32[1024,256]{1,0:T(8,128)} %f_ref.1) | copy-start | bytes 3145732
  91.1 0.8 copy-start.1
  91.9 0.8 copy-start.3
  92.7 0.6 copy-start.4

commit v2 on v1

v2 whole, which is shorter than its diff:
```python
import jax
import jax.numpy as jnp
from jax import lax
from jax.experimental import pallas as pl
from jax.experimental.pallas import tpu as pltpu
from jax.sharding import PartitionSpec as P

ROWS = 8192
COLS = 8192
RANK = 256

MESH = pl.DeviceIdType.MESH
HIGHEST = lax.Precision.HIGHEST
F32 = jnp.float32
BF16 = jnp.bfloat16
BLOCK = 64
BLOCKS = RANK // BLOCK
Y, Z, X = 4, 8, 4
STOP = 99
CORE_MIB = 52
FINAL_MIB = 24
CHIPS = X * Y
PLANE = Y * Z
LOCAL = 1024
HALF = LOCAL // 2
OWN = LOCAL // (2 * CHIPS)
PARTS = 8
CHUNK = LOCAL // PARTS
TILE = 128
QUARTER = LOCAL // Y


def dot(a, b):
    return jnp.dot(a, b, precision=HIGHEST, preferred_element_type=F32)


def low_dot(a, b):
    return jnp.dot(a, b, preferred_element_type=F32)


def factor_block(w, size):
    lanes = w.shape[1]
    row = lax.broadcasted_iota(jnp.int32, (8, lanes), 0)
    done = []
    for j in range(0, size, 8):
        v = w[0:8, :]
        p = [jnp.broadcast_to(v[m : m + 1, :], (8, lanes)) for m in range(8)]
        a = [
            [jnp.broadcast_to(p[i][:, j + m : j + m + 1], (8, lanes)) for m in range(i + 1)]
            for i in range(8)
        ]
        rest = w[8:, :]
        n = rest.shape[0]
        columns = [jnp.broadcast_to(rest[:, j + m : j + m + 1], (n, lanes)) for m in range(8)] if n else []
        low = [[None] * 8 for _ in range(8)]
        inverse = [None] * 8
        for k in range(8):
            inverse[k] = 1.0 / a[k][k]
            for i in range(k + 1, 8):
                low[i][k] = a[i][k] * inverse[k]
            for i in range(k + 1, 8):
                for m in range(k + 1, i + 1):
                    a[i][m] = a[i][m] - low[i][k] * a[m][k]
            for i in range(k + 1, 8):
                p[i] = p[i] - low[i][k] * p[k]
        out = p[7] * lax.rsqrt(a[7][7])
        for k in range(6, -1, -1):
            out = jnp.where(row == k, p[k] * lax.rsqrt(a[k][k]), out)
        done.append(out)
        if n:
            q = [None] * 8
            for k in range(7, -1, -1):
                q[k] = p[k] * inverse[k]
                for i in range(7, k, -1):
                    q[k] = q[k] - low[i][k] * q[i]
            for k in range(8):
                rest = rest - columns[k] * jnp.broadcast_to(q[k][0:1, :], (n, lanes))
            w = rest
    return jnp.concatenate(done, axis=0)


def eliminate(gram, inv, block):
    lo, hi = block * BLOCK, (block + 1) * BLOCK
    rows = gram[lo:hi, :]
    r_i = lax.broadcasted_iota(jnp.int32, (BLOCK, BLOCK), 0)
    c_i = lax.broadcasted_iota(jnp.int32, (BLOCK, BLOCK), 1)
    eye = jnp.where(r_i == c_i, 1.0, 0.0).astype(F32)
    root = factor_block(jnp.concatenate([rows[:, lo:hi], eye], axis=1), BLOCK)[:, BLOCK:]
    mine = dot(root, inv[lo:hi, :])
    inv[lo:hi, :] = mine
    if hi < RANK:
        upper = dot(root, rows)
        below = upper.T[hi:, :]
        gram[hi:, :] = gram[hi:, :] - dot(below, upper)
        inv[hi:, :] = inv[hi:, :] - dot(below, mine)
    return mine


def remote(src, dst, send, recv, **where):
    return pltpu.make_async_remote_copy(
        src_ref=src, dst_ref=dst, send_sem=send, recv_sem=recv, device_id=where, device_id_type=MESH
    )


def take(ref, sem):
    pltpu.make_async_copy(ref, ref, sem).wait()


def hops(step, size):
    return min(step, size - step)


def by_distance(*sizes):
    steps = [()]
    for size in sizes:
        steps = [s + (i,) for s in steps for i in range(size)]
    far = lambda s: sum(hops(a, n) for a, n in zip(s, sizes) if n > 2)
    return sorted([s for s in steps if any(s)], key=far, reverse=True)


CHIP_STEPS = by_distance(Y, X)
PLANE_STEPS = by_distance(Y, X, 2)
LINE_STEPS = by_distance(Y, Z)
Z_STEPS = by_distance(Z)
X_STEPS = by_distance(X, 2)


def core_kernel(
    m_hbm, g_hbm, f_hbm,
    ortho, right_t, scale,
    mv, gv, ff, fv, part, partner_in, half, outgoing, incoming, left, left_t,
    gram, gram_in, line_in, gram_all, work, inv, rs_out, rs_in, spread, square_in,
    load_sem, pair_sem, rs_sem, ag_send, ag_recv, fw_send, fw_recv, gr_sem,
    z_sem, gg_send, gg_recv, gf_send, gf_recv, r_send, r_recv, s_send, s_recv, n_send, n_recv,
):
    y = lax.axis_index("dp")
    z = lax.axis_index("fsdp")
    t = lax.axis_index("tensor")
    x = t // 2
    c = lax.rem(t, 2)
    other = t + 1 - 2 * c
    me = c * CHIPS + y * X + x
    seat = y * Z + z
    own_base = c * HALF
    other_base = HALF - own_base

    def first_row(i):
        base = other_base if i < PARTS // 2 else own_base
        return pl.multiple_of(base + (i % (PARTS // 2)) * CHUNK, CHUNK)

    def load(i, which):
        src, dst = ((m_hbm, mv), (g_hbm, gv))[which]
        rows = pl.ds(first_row(i), CHUNK)
        return pltpu.make_async_copy(src.at[rows, :], dst.at[rows, :], load_sem.at[which, i])

    load_factor = pltpu.make_async_copy(f_hbm, ff, load_sem.at[2, 0])
    load_factor.start()
    for i in range(PARTS):
        load(i, 0).start()
        load(i, 1).start()

    def wrap(a, step, size):
        return lax.rem(a + step, size) if step else a

    def chip_at(step, back=False):
        dy, dx = step
        if back:
            dy, dx = (Y - dy) % Y, (X - dx) % X
        return wrap(y, dy, Y), wrap(x, dx, X)

    barrier = pltpu.get_barrier_semaphore()

    def greet(**where):
        pl.semaphore_signal(barrier, inc=1, device_id=where, device_id_type=MESH)

    for dy, dz in LINE_STEPS:
        greet(dp=wrap(y, dy, Y), fsdp=wrap(z, dz, Z), tensor=t)
    for dy, dx, dc in PLANE_STEPS:
        greet(dp=wrap(y, dy, Y), fsdp=z, tensor=wrap(x, dx, X) * 2 + wrap(c, dc, 2))

    pending = []

    def finish():
        for wait in pending:
            wait()

    load_factor.wait()
    fv[...] = ff[...].astype(BF16)
    for i in range(PARTS):
        load(i, 0).wait()
        load(i, 1).wait()
        rows = pl.ds(first_row(i), CHUNK)
        part[i * CHUNK : (i + 1) * CHUNK, :] = low_dot(mv[rows, :], fv[...]) + low_dot(gv[rows, :], fv[...])

    pl.semaphore_wait(barrier, len(LINE_STEPS) + len(PLANE_STEPS))
    if STOP == 1:
        return finish()
    to_partner = remote(part.at[0:HALF, :], partner_in, pair_sem.at[0], pair_sem.at[1], dp=y, fsdp=z, tensor=other)
    to_partner.start()
    pending.append(to_partner.wait_send)
    to_partner.wait_recv()
    both = (part[HALF:, :] + partner_in[...]).reshape(CHIPS, OWN, RANK)
    half[...] = both
    outgoing[...] = both.astype(BF16)

    for i, step in enumerate(CHIP_STEPS):
        py, px = chip_at(step)
        remote(outgoing.at[py * X + px], incoming.at[i], rs_sem.at[0], rs_sem.at[1], dp=py, fsdp=z, tensor=px * 2 + c).start()
    pending.append(lambda: take(incoming, rs_sem.at[0]))
    take(incoming, rs_sem.at[1])
    if STOP == 2:
        return finish()
    mine = half[y * X + x]
    for i in range(CHIPS - 1):
        mine = mine + incoming[i].astype(F32)
    mine = mine * 0.25
    left[me] = mine

    gram[...] = dot(mine.T, mine).reshape(2 * CHIPS, 8, RANK)
    for i, (dy, dx, dc) in enumerate(PLANE_STEPS):
        py, px, pc = wrap(y, dy, Y), wrap(x, dx, X), wrap(c, dc, 2)
        remote(gram.at[pc * CHIPS + py * X + px], gram_in.at[i], gr_sem.at[0], gr_sem.at[1], dp=py, fsdp=z, tensor=px * 2 + pc).start()
    pending.append(lambda: take(gram_in, gr_sem.at[0]))

    left_copies = []
    for i, step in enumerate(CHIP_STEPS):
        py, px = chip_at(step)
        copy = remote(left.at[me], left.at[me], ag_send.at[i], ag_recv.at[i], dp=py, fsdp=z, tensor=px * 2 + c)
        copy.start()
        left_copies.append(copy)
        pending.append(copy.wait_send)

    def forward(ref, send, recv, i, step):
        py, px = chip_at(step, back=True)
        slot = c * CHIPS + py * X + px
        copy = remote(ref.at[slot], ref.at[slot], send.at[i], recv.at[i], dp=y, fsdp=z, tensor=other)
        copy.start()
        pending.append(copy.wait_send)
        return copy

    left_forwards = [forward(left, fw_send, fw_recv, CHIPS - 1, (0, 0))]

    take(gram_in, gr_sem.at[1])
    if STOP == 3:
        for copy in left_copies:
            copy.wait_recv()
        left_forwards[0].wait_recv()
        return finish()
    mine = gram[me]
    for i in range(2 * CHIPS - 1):
        mine = mine + gram_in[i]
    gram[me] = mine

    for i, (dz,) in enumerate(Z_STEPS):
        remote(gram.at[me], line_in.at[i], z_sem.at[0], z_sem.at[1], dp=y, fsdp=wrap(z, dz, Z), tensor=t).start()
    pending.append(lambda: take(line_in, z_sem.at[0]))
    take(line_in, z_sem.at[1])
    for i in range(Z - 1):
        mine = mine + line_in[i]
    gram_all[me] = mine

    gram_copies = []
    for i, step in enumerate(CHIP_STEPS):
        py, px = chip_at(step)
        copy = remote(gram_all.at[me], gram_all.at[me], gg_send.at[i], gg_recv.at[i], dp=py, fsdp=z, tensor=px * 2 + c)
        copy.start()
        gram_copies.append(copy)
        pending.append(copy.wait_send)
    gram_forwards = [forward(gram_all, gf_send, gf_recv, CHIPS - 1, (0, 0))]
    if STOP == 4:
        for copy in left_copies + gram_copies:
            copy.wait_recv()
        left_forwards[0].wait_recv()
        gram_forwards[0].wait_recv()
        return finish()

    for i in range(CHIPS - 2, -1, -1):
        left_copies[i].wait_recv()
        left_forwards.append(forward(left, fw_send, fw_recv, i, CHIP_STEPS[i]))
    for copy in left_forwards:
        copy.wait_recv()
    left_t[...] = left[...].reshape(LOCAL, RANK).T
    for i in range(CHIPS - 2, -1, -1):
        gram_copies[i].wait_recv()
        gram_forwards.append(forward(gram_all, gf_send, gf_recv, i, CHIP_STEPS[i]))
    for copy in gram_forwards:
        copy.wait_recv()
    if STOP == 5:
        return finish()

    work[...] = gram_all[...].reshape(RANK, RANK)
    r_i = lax.broadcasted_iota(jnp.int32, (RANK, RANK), 0)
    c_i = lax.broadcasted_iota(jnp.int32, (RANK, RANK), 1)
    inv[...] = jnp.where(r_i == c_i, 1.0, 0.0).astype(F32)

    def right_sum(b):
        take(rs_in.at[b], r_recv.at[b])
        mine = rs_out[b, seat].astype(F32)
        for i in range(PLANE - 1):
            mine = mine + rs_in[b, i].astype(F32)
        spread[b, seat] = (mine * 0.25).astype(BF16)
        slot = spread.at[b, seat]
        for dy, dz in LINE_STEPS:
            remote(slot, slot, s_send.at[b], s_recv.at[b], dp=wrap(y, dy, Y), fsdp=wrap(z, dz, Z), tensor=t).start()
        pending.append(lambda: take(rs_in.at[b], s_send.at[b]))

    k_i = lax.broadcasted_iota(jnp.int32, (BLOCK, TILE), 0)
    l_i = lax.broadcasted_iota(jnp.int32, (BLOCK, TILE), 1)

    def collect(b):
        take(rs_in.at[b], s_recv.at[b])
        squares = jnp.zeros((BLOCK, QUARTER), F32)
        for py in range(Y):
            piece = jnp.concatenate([spread[b, py * Z + pz].astype(F32) for pz in range(Z)], axis=0)
            right_t[b * BLOCK : (b + 1) * BLOCK, py * QUARTER : (py + 1) * QUARTER] = piece.astype(BF16)
            squares = squares + piece * piece
        column = jnp.sum(squares, axis=1, keepdims=True)
        line = jnp.sum(jnp.where(k_i == l_i, column, 0.0), axis=0, keepdims=True)
        square_in[b, t] = jnp.broadcast_to(line, (8, TILE))
        for dx, dc in X_STEPS:
            slot = square_in.at[b, t]
            remote(slot, slot, n_send.at[b], n_recv.at[b], dp=y, fsdp=z, tensor=wrap(x, dx, X) * 2 + wrap(c, dc, 2)).start()
        pending.append(lambda: take(square_in.at[b, 1:], n_send.at[b]))

    def norm(b):
        take(square_in.at[b, 1:], n_recv.at[b])
        sums = square_in[b, 0]
        for i in range(1, 2 * X):
            sums = sums + square_in[b, i]
        column = jnp.sum(jnp.where(k_i == l_i, sums[0:1, :], 0.0), axis=1, keepdims=True)
        scale[b * BLOCK : (b + 1) * BLOCK, :] = jnp.broadcast_to(lax.rsqrt(column * (1.0 / COLS) + 1e-06), (BLOCK, TILE))

    for b in range(BLOCKS):
        rows_of = eliminate(work, inv, b)
        wide = dot(rows_of, left_t[...])
        low = wide.astype(BF16)
        term = low_dot(low, mv[...]) + low_dot(low, gv[...])
        for pz in range(Z):
            for py in range(Y):
                rs_out[b, py * Z + pz] = term[pz * 8 : pz * 8 + 8, py * QUARTER : (py + 1) * QUARTER].astype(BF16)
        for i, (dy, dz) in enumerate(LINE_STEPS):
            py, pz = wrap(y, dy, Y), wrap(z, dz, Z)
            remote(rs_out.at[b, py * Z + pz], rs_in.at[b, i], r_send.at[b], r_recv.at[b], dp=py, fsdp=pz, tensor=t).start()
        pending.append(lambda b=b: take(rs_in.at[b], r_send.at[b]))
        ortho[:, b * BLOCK : (b + 1) * BLOCK] = wide.T.astype(BF16)
        if b >= 2:
            right_sum(b - 2)
    if STOP == 6:
        for b in (2, 3):
            take(rs_in.at[b], r_recv.at[b])
        for b in (0, 1):
            take(rs_in.at[b], s_recv.at[b])
        return finish()
    collect(0)
    right_sum(2)
    collect(1)
    norm(0)
    right_sum(3)
    collect(2)
    norm(1)
    norm(2)
    if STOP == 7:
        take(rs_in.at[3], s_recv.at[3])
        return finish()
    collect(3)
    norm(3)
    finish()


def core(moment, change, factor):
    vmem = pl.BlockSpec(memory_space=pltpu.VMEM)
    hbm = pl.BlockSpec(memory_space=pltpu.HBM)
    dma = pltpu.SemaphoreType.DMA
    return pl.pallas_call(
        core_kernel,
        out_shape=(
            jax.ShapeDtypeStruct((LOCAL, RANK), BF16),
            jax.ShapeDtypeStruct((RANK, LOCAL), BF16),
            jax.ShapeDtypeStruct((RANK, TILE), F32),
        ),
        in_specs=[hbm, hbm, hbm],
        out_specs=(vmem, vmem, vmem),
        scratch_shapes=[
            pltpu.VMEM((LOCAL, LOCAL), BF16),
            pltpu.VMEM((LOCAL, LOCAL), BF16),
            pltpu.VMEM((LOCAL, RANK), F32),
            pltpu.VMEM((LOCAL, RANK), BF16),
            pltpu.VMEM((LOCAL, RANK), F32),
            pltpu.VMEM((HALF, RANK), F32),
            pltpu.VMEM((CHIPS, OWN, RANK), F32),
            pltpu.VMEM((CHIPS, OWN, RANK), BF16),
            pltpu.VMEM((CHIPS - 1, OWN, RANK), BF16),
            pltpu.VMEM((2 * CHIPS, OWN, RANK), F32),
            pltpu.VMEM((RANK, LOCAL), F32),
            pltpu.VMEM((2 * CHIPS, 8, RANK), F32),
            pltpu.VMEM((2 * CHIPS - 1, 8, RANK), F32),
            pltpu.VMEM((Z - 1, 8, RANK), F32),
            pltpu.VMEM((2 * CHIPS, 8, RANK), F32),
            pltpu.VMEM((RANK, RANK), F32),
            pltpu.VMEM((RANK, RANK), F32),
            pltpu.VMEM((BLOCKS, PLANE, 8, QUARTER), BF16),
            pltpu.VMEM((BLOCKS, PLANE - 1, 8, QUARTER), BF16),
            pltpu.VMEM((BLOCKS, PLANE, 8, QUARTER), BF16),
            pltpu.VMEM((BLOCKS, 2 * X, 8, TILE), F32),
            dma((3, PARTS)),
            dma((2,)),
            dma((2,)),
            dma((CHIPS,)),
            dma((CHIPS,)),
            dma((CHIPS,)),
            dma((CHIPS,)),
            dma((2,)),
            dma((2,)),
            dma((CHIPS,)),
            dma((CHIPS,)),
            dma((CHIPS,)),
            dma((CHIPS,)),
            dma((BLOCKS,)),
            dma((BLOCKS,)),
            dma((BLOCKS,)),
            dma((BLOCKS,)),
            dma((BLOCKS,)),
            dma((BLOCKS,)),
        ],
        compiler_params=pltpu.CompilerParams(
            collective_id=0, has_side_effects=True, vmem_limit_bytes=CORE_MIB * 1024 * 1024
        ),
    )(moment, change, factor)


def final_kernel(m_ref, g_ref, o_ref, r_ref, s_ref, nm_ref, sd_ref, nf_ref, fv):
    i = pl.program_id(0)

    @pl.when(i == 0)
    def _():
        fv[...] = (r_ref[...].astype(F32) * s_ref[:, 0:1]).astype(BF16)

    rows = pl.ds(pl.multiple_of(i * TILE, TILE), TILE)
    low = o_ref[rows, :]
    nm_ref[...] = m_ref[...].astype(F32) + g_ref[...].astype(F32) - 0.05 * low_dot(low, r_ref[...])
    sd_ref[...] = (jnp.sqrt(F32(ROWS / RANK)) * low_dot(low, fv[...])).astype(BF16)
    nf_ref[...] = (r_ref[:, rows].astype(F32) * s_ref[...]).T


def final(moment, change, ortho, right_t, scale):
    row = lambda i: (i, 0)
    vmem = pl.BlockSpec(memory_space=pltpu.VMEM)
    return pl.pallas_call(
        final_kernel,
        grid=(LOCAL // TILE,),
        out_shape=(
            jax.ShapeDtypeStruct((LOCAL, LOCAL), F32),
            jax.ShapeDtypeStruct((LOCAL, LOCAL), BF16),
            jax.ShapeDtypeStruct((LOCAL, RANK), F32),
        ),
        in_specs=[pl.BlockSpec((TILE, LOCAL), row), pl.BlockSpec((TILE, LOCAL), row), vmem, vmem, vmem],
        out_specs=(
            pl.BlockSpec((TILE, LOCAL), row),
            pl.BlockSpec((TILE, LOCAL), row),
            pl.BlockSpec((TILE, RANK), row),
        ),
        scratch_shapes=[pltpu.VMEM((RANK, LOCAL), BF16)],
        compiler_params=pltpu.CompilerParams(vmem_limit_bytes=FINAL_MIB * 1024 * 1024),
    )(moment, change, ortho, right_t, scale)


def local(momentum, gradient, factor):
    new_momentum, step_direction, new_factor = final(momentum[0], gradient[0], *core(momentum[0], gradient[0], factor))
    return new_momentum[None], step_direction, new_factor


def solution(mesh):
    in_specs = (P("dp", "fsdp", "tensor"), P("dp", "fsdp", "tensor"), P("tensor", None))
    out_specs = (P("dp", "fsdp", "tensor"), P("fsdp", "tensor"), P("tensor", None))
    return jax.shard_map(local, mesh=mesh, in_specs=in_specs, out_specs=out_specs, check_vma=False)
```

time: 103 us -> 84.5 us (0.82)
  Pallas kernels: 96.8 us -> 83.7 us
  local copies, waits for them, and re-layouts: 4.98 us -> 0.01 us
    pallas_call x2, Pallas kernels: 96.8 us -> 83.7 us  [the longest x1 78.5 us: core(): pl.pallas_call(core_kernel, out_shape=(jax.ShapeDtypeStruct((LOCAL, RANK)...]
    unnamed x10 -> x4, local copies, waits for them, and re-layouts: 4.98 us -> 0.01 us
where the time goes in v2:
time: 84.5 us; the launch traced here: 84.4 us
  Pallas kernels  83.7 us (99%)
    pallas_call x1, Pallas kernels, core(): pl.pallas_call(core_kernel, out_shape=(jax.ShapeDtypeStruct((LOCAL, RANK)...  78.5 us
    pallas_call x1, Pallas kernels, final(): pl.pallas_call(final_kernel, grid=(LOCAL // TILE,), out_shape=(jax.ShapeD...  5.2 us

profile of v2, /device:TPU:1, one launch (start us, length us, event | category | flops | bytes accessed | tf_op | source)
XLA Modules:
  0.0 84.4 jit_solution(8096349405861529180)
XLA Ops:
  0.6 0.0 copy-start
  0.6 0.0 copy-start.1
  0.7 78.5 %shard_map.58 = (bf16[1024,256]{1,0:T(8,128)(2,1)S(1)}, bf16[256,1024]{1,0:T(8,128)(2,1)S(1)}, f32[256,128]{1,0:T(8,128)S(1)}) custom-call(bf16[1024,1024]{1,0:T(8,128)(2,1)} %bitcast.3, bf16[1024,1024]{1,0:T(8,128)(2,1)} %bitcast.5, f32[1024,256]{1,0:T(8,128)} %f_hbm.1), custom_call_target="tpu_custom_call" | custom-call | tf_op jit(solution)/shard_map/pallas_call | solution.py:374
  79.2 0.0 copy-done
  79.2 0.0 copy-done.1
  79.2 5.2 %shard_map.59 = (f32[1024,1024]{1,0:T(8,128)}, bf16[1024,1024]{1,0:T(8,128)(2,1)}, f32[1024,256]{1,0:T(8,128)}) custom-call(bf16[1024,1024]{1,0:T(8,128)(2,1)S(1)} %bitcast.4, bf16[1024,1024]{1,0:T(8,128)(2,1)S(1)} %bitcast.6, bf16[1024,256]{1,0:T(8,128)(2,1)S(1)} %get-tuple-element.9.o_ref, bf16[256,1024]{1,0:T(8,128)(2,1)S(1)} %get-tuple-element.10.r_ref, ...), custom_call_target="tpu_custom_call" | custom-call | tf_op jit(solution)/shard_map/pallas_call | solution.py:448
Async XLA Ops:
  0.6 78.5 %copy-start = (bf16[1,1024,1024]{2,1,0:T(8,128)(2,1)S(1)}, bf16[1,1024,1024]{2,1,0:T(8,128)(2,1)}, u32[]{:S(2)}) copy-start(bf16[1,1024,1024]{2,1,0:T(8,128)(2,1)} %param.3) | copy-start | bytes 6291460
  0.6 78.5 %copy-start.1 = (bf16[1,1024,1024]{2,1,0:T(8,128)(2,1)S(1)}, bf16[1,1024,1024]{2,1,0:T(8,128)(2,1)}, u32[]{:S(2)}) copy-start(bf16[1,1024,1024]{2,1,0:T(8,128)(2,1)} %param.4) | copy-start | bytes 6291460

commit v3 on v2

--- a/solution.py
+++ b/solution.py
@@ -24,9 +24,10 @@
 LOCAL = 1024
 HALF = LOCAL // 2
 OWN = LOCAL // (2 * CHIPS)
-PARTS = 8
+PARTS = 4
 CHUNK = LOCAL // PARTS
 TILE = 128
+WIDE = 256
 QUARTER = LOCAL // Y
 
 
@@ -122,16 +123,17 @@
 PLANE_STEPS = by_distance(Y, X, 2)
 LINE_STEPS = by_distance(Y, Z)
 Z_STEPS = by_distance(Z)
+Y_STEPS = by_distance(Y)
 X_STEPS = by_distance(X, 2)
 
 
 def core_kernel(
     m_hbm, g_hbm, f_hbm,
     ortho, right_t, scale,
-    mv, gv, ff, fv, part, partner_in, half, outgoing, incoming, left, left_t,
-    gram, gram_in, line_in, gram_all, work, inv, rs_out, rs_in, spread, square_in,
+    mv, gv, sv, ff, fv, part, partner_in, half, outgoing, incoming, left, left_hi, left_lo, wide_t,
+    gram, gram_in, line_in, gram_all, work, inv, rs_out, rs_in, y_in, y_sum, z_in, spread, square_in,
     load_sem, pair_sem, rs_sem, ag_send, ag_recv, fw_send, fw_recv, gr_sem,
-    z_sem, gg_send, gg_recv, gf_send, gf_recv, r_send, r_recv, s_send, s_recv, n_send, n_recv,
+    z_sem, gg_sem, r_send, r_recv, s_send, s_recv, n_send, n_recv, y_sem, z2_sem,
 ):
     y = lax.axis_index("dp")
     z = lax.axis_index("fsdp")
@@ -144,6 +146,19 @@
     own_base = c * HALF
     other_base = HALF - own_base
 
+    def wrap(a, step, size):
+        return lax.rem(a + step, size) if step else a
+
+    barrier = pltpu.get_barrier_semaphore()
+
+    def greet(**where):
+        pl.semaphore_signal(barrier, inc=1, device_id=where, device_id_type=MESH)
+
+    for dy, dz in LINE_STEPS:
+        greet(dp=wrap(y, dy, Y), fsdp=wrap(z, dz, Z), tensor=t)
+    for dy, dx, dc in PLANE_STEPS:
+        greet(dp=wrap(y, dy, Y), fsdp=z, tensor=wrap(x, dx, X) * 2 + wrap(c, dc, 2))
+
     def first_row(i):
         base = other_base if i < PARTS // 2 else own_base
         return pl.multiple_of(base + (i % (PARTS // 2)) * CHUNK, CHUNK)
@@ -159,24 +174,11 @@
         load(i, 0).start()
         load(i, 1).start()
 
-    def wrap(a, step, size):
-        return lax.rem(a + step, size) if step else a
-
     def chip_at(step, back=False):
         dy, dx = step
         if back:
             dy, dx = (Y - dy) % Y, (X - dx) % X
         return wrap(y, dy, Y), wrap(x, dx, X)
-
-    barrier = pltpu.get_barrier_semaphore()
-
-    def greet(**where):
-        pl.semaphore_signal(barrier, inc=1, device_id=where, device_id_type=MESH)
-
-    for dy, dz in LINE_STEPS:
-        greet(dp=wrap(y, dy, Y), fsdp=wrap(z, dz, Z), tensor=t)
-    for dy, dx, dc in PLANE_STEPS:
-        greet(dp=wrap(y, dy, Y), fsdp=z, tensor=wrap(x, dx, X) * 2 + wrap(c, dc, 2))
 
     pending = []
 
@@ -207,6 +209,11 @@
         py, px = chip_at(step)
         remote(outgoing.at[py * X + px], incoming.at[i], rs_sem.at[0], rs_sem.at[1], dp=py, fsdp=z, tensor=px * 2 + c).start()
     pending.append(lambda: take(incoming, rs_sem.at[0]))
+
+    @pl.when(t >= 0)
+    def _():
+        sv[...] = (mv[...].astype(F32) + gv[...].astype(F32)).astype(BF16)
+
     take(incoming, rs_sem.at[1])
     if STOP == 2:
         return finish()
@@ -222,6 +229,24 @@
         remote(gram.at[pc * CHIPS + py * X + px], gram_in.at[i], gr_sem.at[0], gr_sem.at[1], dp=py, fsdp=z, tensor=px * 2 + pc).start()
     pending.append(lambda: take(gram_in, gr_sem.at[0]))
 
+    def forward(ref, send, recv, i, step):
+        py, px = chip_at(step, back=True)
+        slot = c * CHIPS + py * X + px
+        copy = remote(ref.at[slot], ref.at[slot], send.at[i], recv.at[i], dp=y, fsdp=z, tensor=other)
+        copy.start()
+        pending.append(copy.wait_send)
+        return copy
+
+    take(gram_in, gr_sem.at[1])
+    mine = gram[me]
+    for i in range(2 * CHIPS - 1):
+        mine = mine + gram_in[i]
+    gram[me] = mine
+
+    for i, (dz,) in enumerate(Z_STEPS):
+        remote(gram.at[me], line_in.at[i], z_sem.at[0], z_sem.at[1], dp=y, fsdp=wrap(z, dz, Z), tensor=t).start()
+    pending.append(lambda: take(line_in, z_sem.at[0]))
+
     left_copies = []
     for i, step in enumerate(CHIP_STEPS):
         py, px = chip_at(step)
@@ -229,86 +254,99 @@
         copy.start()
         left_copies.append(copy)
         pending.append(copy.wait_send)
-
-    def forward(ref, send, recv, i, step):
-        py, px = chip_at(step, back=True)
-        slot = c * CHIPS + py * X + px
-        copy = remote(ref.at[slot], ref.at[slot], send.at[i], recv.at[i], dp=y, fsdp=z, tensor=other)
-        copy.start()
-        pending.append(copy.wait_send)
-        return copy
-
     left_forwards = [forward(left, fw_send, fw_recv, CHIPS - 1, (0, 0))]
 
-    take(gram_in, gr_sem.at[1])
-    if STOP == 3:
-        for copy in left_copies:
-            copy.wait_recv()
-        left_forwards[0].wait_recv()
-        return finish()
-    mine = gram[me]
-    for i in range(2 * CHIPS - 1):
-        mine = mine + gram_in[i]
-    gram[me] = mine
-
-    for i, (dz,) in enumerate(Z_STEPS):
-        remote(gram.at[me], line_in.at[i], z_sem.at[0], z_sem.at[1], dp=y, fsdp=wrap(z, dz, Z), tensor=t).start()
-    pending.append(lambda: take(line_in, z_sem.at[0]))
     take(line_in, z_sem.at[1])
     for i in range(Z - 1):
         mine = mine + line_in[i]
     gram_all[me] = mine
 
-    gram_copies = []
-    for i, step in enumerate(CHIP_STEPS):
-        py, px = chip_at(step)
-        copy = remote(gram_all.at[me], gram_all.at[me], gg_send.at[i], gg_recv.at[i], dp=py, fsdp=z, tensor=px * 2 + c)
-        copy.start()
-        gram_copies.append(copy)
-        pending.append(copy.wait_send)
-    gram_forwards = [forward(gram_all, gf_send, gf_recv, CHIPS - 1, (0, 0))]
-    if STOP == 4:
-        for copy in left_copies + gram_copies:
-            copy.wait_recv()
-        left_forwards[0].wait_recv()
-        gram_forwards[0].wait_recv()
-        return finish()
+    slot = gram_all.at[me]
+    for dy, dx, dc in PLANE_STEPS:
+        remote(slot, slot, gg_sem.at[0], gg_sem.at[1], dp=wrap(y, dy, Y), fsdp=z, tensor=wrap(x, dx, X) * 2 + wrap(c, dc, 2)).start()
+    pending.append(lambda: take(gram_in, gg_sem.at[0]))
 
     for i in range(CHIPS - 2, -1, -1):
         left_copies[i].wait_recv()
         left_forwards.append(forward(left, fw_send, fw_recv, i, CHIP_STEPS[i]))
     for copy in left_forwards:
         copy.wait_recv()
-    left_t[...] = left[...].reshape(LOCAL, RANK).T
-    for i in range(CHIPS - 2, -1, -1):
-        gram_copies[i].wait_recv()
-        gram_forwards.append(forward(gram_all, gf_send, gf_recv, i, CHIP_STEPS[i]))
-    for copy in gram_forwards:
-        copy.wait_recv()
+
+    @pl.when(t >= 0)
+    def _():
+        flat = left[...].reshape(LOCAL, RANK).T
+        left_hi[...] = flat.astype(BF16)
+        left_lo[...] = (flat - flat.astype(BF16).astype(F32)).astype(BF16)
+
+    take(gram_in, gg_sem.at[1])
     if STOP == 5:
         return finish()
-
     work[...] = gram_all[...].reshape(RANK, RANK)
     r_i = lax.broadcasted_iota(jnp.int32, (RANK, RANK), 0)
     c_i = lax.broadcasted_iota(jnp.int32, (RANK, RANK), 1)
     inv[...] = jnp.where(r_i == c_i, 1.0, 0.0).astype(F32)
 
-    def right_sum(b):
-        take(rs_in.at[b], r_recv.at[b])
-        mine = rs_out[b, seat].astype(F32)
-        for i in range(PLANE - 1):
-            mine = mine + rs_in[b, i].astype(F32)
+    last = BLOCKS - 1
+
+    def send_right(b):
+        if b == last:
+            for i, (dy, dz) in enumerate(LINE_STEPS):
+                py, pz = wrap(y, dy, Y), wrap(z, dz, Z)
+                remote(rs_out.at[b, py * Z + pz], rs_in.at[i], r_send.at[b], r_recv.at[b], dp=py, fsdp=pz, tensor=t).start()
+            pending.append(lambda: take(rs_in, r_send.at[b]))
+            return
+        for i, (dy,) in enumerate(Y_STEPS):
+            py = wrap(y, dy, Y)
+            remote(rs_out.at[b, pl.ds(py * Z, Z)], y_in.at[b, i], r_send.at[b], r_recv.at[b], dp=py, fsdp=z, tensor=t).start()
+        pending.append(lambda: take(y_in.at[b], r_send.at[b]))
+
+    def sum_y(b):
+        take(y_in.at[b], r_recv.at[b])
+        sums = rs_out[b, pl.ds(y * Z, Z)].astype(F32)
+        for i in range(Y - 1):
+            sums = sums + y_in[b, i].astype(F32)
+        y_sum[b] = sums.astype(BF16)
+        for i, (dz,) in enumerate(Z_STEPS):
+            pz = wrap(z, dz, Z)
+            remote(y_sum.at[b, pz], z_in.at[b, i], z2_sem.at[0, b], z2_sem.at[1, b], dp=y, fsdp=pz, tensor=t).start()
+        pending.append(lambda: take(z_in.at[b], z2_sem.at[0, b]))
+
+    def sum_z(b):
+        slot = spread.at[b, seat]
+        if b == last:
+            take(rs_in, r_recv.at[b])
+            mine = rs_out[b, seat].astype(F32)
+            for i in range(PLANE - 1):
+                mine = mine + rs_in[i].astype(F32)
+            spread[b, seat] = (mine * 0.25).astype(BF16)
+            for dy, dz in LINE_STEPS:
+                remote(slot, slot, s_send.at[b], s_recv.at[b], dp=wrap(y, dy, Y), fsdp=wrap(z, dz, Z), tensor=t).start()
+            pending.append(lambda: take(rs_in, s_send.at[b]))
+            return
+        take(z_in.at[b], z2_sem.at[1, b])
+        mine = y_sum[b, z].astype(F32)
+        for i in range(Z - 1):
+            mine = mine + z_in[b, i].astype(F32)
         spread[b, seat] = (mine * 0.25).astype(BF16)
-        slot = spread.at[b, seat]
-        for dy, dz in LINE_STEPS:
-            remote(slot, slot, s_send.at[b], s_recv.at[b], dp=wrap(y, dy, Y), fsdp=wrap(z, dz, Z), tensor=t).start()
-        pending.append(lambda: take(rs_in.at[b], s_send.at[b]))
+        for (dz,) in Z_STEPS:
+            remote(slot, slot, s_send.at[b], s_recv.at[b], dp=y, fsdp=wrap(z, dz, Z), tensor=t).start()
+        pending.append(lambda: take(z_in.at[b], s_send.at[b]))
+
+    def spread_y(b):
+        take(z_in.at[b], s_recv.at[b])
+        line = spread.at[b, pl.ds(y * Z, Z)]
+        for (dy,) in Y_STEPS:
+            remote(line, line, y_sem.at[0, b], y_sem.at[1, b], dp=wrap(y, dy, Y), fsdp=z, tensor=t).start()
+        pending.append(lambda: take(y_in.at[b], y_sem.at[0, b]))
 
     k_i = lax.broadcasted_iota(jnp.int32, (BLOCK, TILE), 0)
     l_i = lax.broadcasted_iota(jnp.int32, (BLOCK, TILE), 1)
 
     def collect(b):
-        take(rs_in.at[b], s_recv.at[b])
+        if b == last:
+            take(rs_in, s_recv.at[b])
+        else:
+            take(y_in.at[b], y_sem.at[1, b])
         squares = jnp.zeros((BLOCK, QUARTER), F32)
         for py in range(Y):
             piece = jnp.concatenate([spread[b, py * Z + pz].astype(F32) for pz in range(Z)], axis=0)
@@ -330,40 +368,45 @@
         column = jnp.sum(jnp.where(k_i == l_i, sums[0:1, :], 0.0), axis=1, keepdims=True)
         scale[b * BLOCK : (b + 1) * BLOCK, :] = jnp.broadcast_to(lax.rsqrt(column * (1.0 / COLS) + 1e-06), (BLOCK, TILE))
 
-    for b in range(BLOCKS):
+    def compute(b):
         rows_of = eliminate(work, inv, b)
-        wide = dot(rows_of, left_t[...])
+        first = rows_of.astype(BF16)
+        second = (rows_of - first.astype(F32)).astype(BF16)
+        twice = low_dot(jnp.concatenate([first, second], axis=0), left_hi[...])
+        wide = twice[:BLOCK] + twice[BLOCK:] + low_dot(first, left_lo[...])
         low = wide.astype(BF16)
-        term = low_dot(low, mv[...]) + low_dot(low, gv[...])
+        wide_t[b * BLOCK : (b + 1) * BLOCK, :] = wide
+        term = low_dot(low, sv[...])
         for pz in range(Z):
             for py in range(Y):
                 rs_out[b, py * Z + pz] = term[pz * 8 : pz * 8 + 8, py * QUARTER : (py + 1) * QUARTER].astype(BF16)
-        for i, (dy, dz) in enumerate(LINE_STEPS):
-            py, pz = wrap(y, dy, Y), wrap(z, dz, Z)
-            remote(rs_out.at[b, py * Z + pz], rs_in.at[b, i], r_send.at[b], r_recv.at[b], dp=py, fsdp=pz, tensor=t).start()
-        pending.append(lambda b=b: take(rs_in.at[b], r_send.at[b]))
-        ortho[:, b * BLOCK : (b + 1) * BLOCK] = wide.T.astype(BF16)
+
+    for b in range(BLOCKS):
+        pl.when(t >= 0)(lambda b=b: compute(b))
+        send_right(b)
+        if b >= 1:
+            sum_y(b - 1)
         if b >= 2:
-            right_sum(b - 2)
-    if STOP == 6:
-        for b in (2, 3):
-            take(rs_in.at[b], r_recv.at[b])
-        for b in (0, 1):
-            take(rs_in.at[b], s_recv.at[b])
-        return finish()
+            sum_z(b - 2)
+        if b >= 3:
+            spread_y(b - 3)
+
+    @pl.when(t >= 0)
+    def _():
+        ortho[...] = wide_t[...].T.astype(BF16)
+
+    sum_z(last - 1)
+    spread_y(last - 2)
     collect(0)
-    right_sum(2)
+    sum_z(last)
+    spread_y(last - 1)
     collect(1)
+    collect(2)
     norm(0)
-    right_sum(3)
-    collect(2)
     norm(1)
+    collect(last)
     norm(2)
-    if STOP == 7:
-        take(rs_in.at[3], s_recv.at[3])
-        return finish()
-    collect(3)
-    norm(3)
+    norm(last)
     finish()
 
 
@@ -383,6 +426,7 @@
         scratch_shapes=[
             pltpu.VMEM((LOCAL, LOCAL), BF16),
             pltpu.VMEM((LOCAL, LOCAL), BF16),
+            pltpu.VMEM((LOCAL, LOCAL), BF16),
             pltpu.VMEM((LOCAL, RANK), F32),
             pltpu.VMEM((LOCAL, RANK), BF16),
             pltpu.VMEM((LOCAL, RANK), F32),
@@ -391,6 +435,8 @@
             pltpu.VMEM((CHIPS, OWN, RANK), BF16),
             pltpu.VMEM((CHIPS - 1, OWN, RANK), BF16),
             pltpu.VMEM((2 * CHIPS, OWN, RANK), F32),
+            pltpu.VMEM((RANK, LOCAL), BF16),
+            pltpu.VMEM((RANK, LOCAL), BF16),
             pltpu.VMEM((RANK, LOCAL), F32),
             pltpu.VMEM((2 * CHIPS, 8, RANK), F32),
             pltpu.VMEM((2 * CHIPS - 1, 8, RANK), F32),
@@ -399,7 +445,10 @@
             pltpu.VMEM((RANK, RANK), F32),
             pltpu.VMEM((RANK, RANK), F32),
             pltpu.VMEM((BLOCKS, PLANE, 8, QUARTER), BF16),
-            pltpu.VMEM((BLOCKS, PLANE - 1, 8, QUARTER), BF16),
+            pltpu.VMEM((PLANE - 1, 8, QUARTER), BF16),
+            pltpu.VMEM((BLOCKS - 1, Y - 1, Z, 8, QUARTER), BF16),
+            pltpu.VMEM((BLOCKS - 1, Z, 8, QUARTER), BF16),
+            pltpu.VMEM((BLOCKS - 1, Z - 1, 8, QUARTER), BF16),
             pltpu.VMEM((BLOCKS, PLANE, 8, QUARTER), BF16),
             pltpu.VMEM((BLOCKS, 2 * X, 8, TILE), F32),
             dma((3, PARTS)),
@@ -411,16 +460,15 @@
             dma((CHIPS,)),
             dma((2,)),
             dma((2,)),
-            dma((CHIPS,)),
-            dma((CHIPS,)),
-            dma((CHIPS,)),
-            dma((CHIPS,)),
+            dma((2,)),
             dma((BLOCKS,)),
             dma((BLOCKS,)),
             dma((BLOCKS,)),
             dma((BLOCKS,)),
             dma((BLOCKS,)),
             dma((BLOCKS,)),
+            dma((2, BLOCKS)),
+            dma((2, BLOCKS)),
         ],
         compiler_params=pltpu.CompilerParams(
             collective_id=0, has_side_effects=True, vmem_limit_bytes=CORE_MIB * 1024 * 1024
@@ -428,38 +476,38 @@
     )(moment, change, factor)
 
 
-def final_kernel(m_ref, g_ref, o_ref, r_ref, s_ref, nm_ref, sd_ref, nf_ref, fv):
-    i = pl.program_id(0)
-
-    @pl.when(i == 0)
-    def _():
-        fv[...] = (r_ref[...].astype(F32) * s_ref[:, 0:1]).astype(BF16)
-
-    rows = pl.ds(pl.multiple_of(i * TILE, TILE), TILE)
-    low = o_ref[rows, :]
-    nm_ref[...] = m_ref[...].astype(F32) + g_ref[...].astype(F32) - 0.05 * low_dot(low, r_ref[...])
-    sd_ref[...] = (jnp.sqrt(F32(ROWS / RANK)) * low_dot(low, fv[...])).astype(BF16)
-    nf_ref[...] = (r_ref[:, rows].astype(F32) * s_ref[...]).T
+def final_kernel(m_ref, g_ref, o_ref, r_ref, s_ref, nm_ref, sd_ref, nf_ref):
+    right = r_ref[...]
+    factor_next = right.astype(F32) * s_ref[:, 0:1]
+    nm_ref[...] = m_ref[...].astype(F32) + g_ref[...].astype(F32) - 0.05 * low_dot(o_ref[...], right)
+    step = low_dot(o_ref[...], factor_next.astype(BF16))
+    sd_ref[...] = (jnp.sqrt(F32(ROWS / RANK)) * step).astype(BF16)
+    nf_ref[...] = factor_next.T
 
 
 def final(moment, change, ortho, right_t, scale):
-    row = lambda i: (i, 0)
+    col = lambda i: (0, i)
     vmem = pl.BlockSpec(memory_space=pltpu.VMEM)
     return pl.pallas_call(
         final_kernel,
-        grid=(LOCAL // TILE,),
+        grid=(LOCAL // WIDE,),
         out_shape=(
             jax.ShapeDtypeStruct((LOCAL, LOCAL), F32),
             jax.ShapeDtypeStruct((LOCAL, LOCAL), BF16),
             jax.ShapeDtypeStruct((LOCAL, RANK), F32),
         ),
-        in_specs=[pl.BlockSpec((TILE, LOCAL), row), pl.BlockSpec((TILE, LOCAL), row), vmem, vmem, vmem],
+        in_specs=[
+            pl.BlockSpec((LOCAL, WIDE), col),
+            pl.BlockSpec((LOCAL, WIDE), col),
+            vmem,
+            pl.BlockSpec((RANK, WIDE), col),
+            vmem,
+        ],
         out_specs=(
-            pl.BlockSpec((TILE, LOCAL), row),
-            pl.BlockSpec((TILE, LOCAL), row),
-            pl.BlockSpec((TILE, RANK), row),
+            pl.BlockSpec((LOCAL, WIDE), col),
+            pl.BlockSpec((LOCAL, WIDE), col),
+            pl.BlockSpec((WIDE, RANK), lambda i: (i, 0)),
         ),
-        scratch_shapes=[pltpu.VMEM((RANK, LOCAL), BF16)],
         compiler_params=pltpu.CompilerParams(vmem_limit_bytes=FINAL_MIB * 1024 * 1024),
     )(moment, change, ortho, right_t, scale)
 

time: 84.5 us -> 78.1 us (0.924)
  Pallas kernels: 83.7 us -> 77.3 us
    pallas_call x1, Pallas kernels: 78.5 us -> 73 us  [core(): pl.pallas_call(core_kernel, out_shape=(jax.ShapeDtypeStruct((LOCAL, RANK)...]
where the time goes in v3:
time: 78.1 us; the launch traced here: 78 us
  Pallas kernels  77.3 us (99%)
    pallas_call x1, Pallas kernels, core(): pl.pallas_call(core_kernel, out_shape=(jax.ShapeDtypeStruct((LOCAL, RANK)...  73 us
    pallas_call x1, Pallas kernels, final(): pl.pallas_call(final_kernel, grid=(LOCAL // WIDE,), out_shape=(jax.ShapeD...  4.36 us

profile of v3, /device:TPU:1, one launch (start us, length us, event | category | flops | bytes accessed | tf_op | source)
XLA Modules:
  0.0 78.0 jit_solution(7302618389280751287)
XLA Ops:
  0.6 0.0 copy-start
  0.6 0.0 copy-start.1
  0.7 73.0 %shard_map.58 = (bf16[1024,256]{1,0:T(8,128)(2,1)S(1)}, bf16[256,1024]{1,0:T(8,128)(2,1)S(1)}, f32[256,128]{1,0:T(8,128)S(1)}) custom-call(bf16[1024,1024]{1,0:T(8,128)(2,1)} %bitcast.3, bf16[1024,1024]{1,0:T(8,128)(2,1)} %bitcast.5, f32[1024,256]{1,0:T(8,128)} %f_hbm.1), custom_call_target="tpu_custom_call" | custom-call | tf_op jit(solution)/shard_map/pallas_call | solution.py:417
  73.6 0.0 copy-done
  73.6 0.0 copy-done.1
  73.7 4.4 %shard_map.59 = (f32[1024,1024]{1,0:T(8,128)}, bf16[1024,1024]{1,0:T(8,128)(2,1)}, f32[1024,256]{1,0:T(8,128)}) custom-call(bf16[1024,1024]{1,0:T(8,128)(2,1)S(1)} %bitcast.4, bf16[1024,1024]{1,0:T(8,128)(2,1)S(1)} %bitcast.6, bf16[1024,256]{1,0:T(8,128)(2,1)S(1)} %get-tuple-element.9.o_ref, bf16[256,1024]{1,0:T(8,128)(2,1)S(1)} %get-tuple-element.10.r_ref, ...), custom_call_target="tpu_custom_call" | custom-call | tf_op jit(solution)/shard_map/pallas_call | solution.py:491
Async XLA Ops:
  0.6 73.0 %copy-start = (bf16[1,1024,1024]{2,1,0:T(8,128)(2,1)S(1)}, bf16[1,1024,1024]{2,1,0:T(8,128)(2,1)}, u32[]{:S(2)}) copy-start(bf16[1,1024,1024]{2,1,0:T(8,128)(2,1)} %param.3) | copy-start | bytes 6291460
  0.6 73.0 %copy-start.1 = (bf16[1,1024,1024]{2,1,0:T(8,128)(2,1)S(1)}, bf16[1,1024,1024]{2,1,0:T(8,128)(2,1)}, u32[]{:S(2)}) copy-start(bf16[1,1024,1024]{2,1,0:T(8,128)(2,1)} %param.4) | copy-start | bytes 6291460

commit v4 on v3

--- a/solution.py
+++ b/solution.py
@@ -27,7 +27,7 @@
 PARTS = 4
 CHUNK = LOCAL // PARTS
 TILE = 128
-WIDE = 256
+WIDE = 512
 QUARTER = LOCAL // Y
 
 
@@ -130,7 +130,7 @@
 def core_kernel(
     m_hbm, g_hbm, f_hbm,
     ortho, right_t, scale,
-    mv, gv, sv, ff, fv, part, partner_in, half, outgoing, incoming, left, left_hi, left_lo, wide_t,
+    mv, gv, sv, ff, fv, part, partner_out, partner_in, half, outgoing, incoming, left, left_hi, left_lo, wide_t,
     gram, gram_in, line_in, gram_all, work, inv, rs_out, rs_in, y_in, y_sum, z_in, spread, square_in,
     load_sem, pair_sem, rs_sem, ag_send, ag_recv, fw_send, fw_recv, gr_sem,
     z_sem, gg_sem, r_send, r_recv, s_send, s_recv, n_send, n_recv, y_sem, z2_sem,
@@ -154,10 +154,10 @@
     def greet(**where):
         pl.semaphore_signal(barrier, inc=1, device_id=where, device_id_type=MESH)
 
-    for dy, dz in LINE_STEPS:
-        greet(dp=wrap(y, dy, Y), fsdp=wrap(z, dz, Z), tensor=t)
     for dy, dx, dc in PLANE_STEPS:
         greet(dp=wrap(y, dy, Y), fsdp=z, tensor=wrap(x, dx, X) * 2 + wrap(c, dc, 2))
+    for (dz,) in Z_STEPS:
+        greet(dp=y, fsdp=wrap(z, dz, Z), tensor=t)
 
     def first_row(i):
         base = other_base if i < PARTS // 2 else own_base
@@ -192,16 +192,20 @@
         load(i, 0).wait()
         load(i, 1).wait()
         rows = pl.ds(first_row(i), CHUNK)
-        part[i * CHUNK : (i + 1) * CHUNK, :] = low_dot(mv[rows, :], fv[...]) + low_dot(gv[rows, :], fv[...])
-
-    pl.semaphore_wait(barrier, len(LINE_STEPS) + len(PLANE_STEPS))
+        product = low_dot(mv[rows, :], fv[...]) + low_dot(gv[rows, :], fv[...])
+        if i < PARTS // 2:
+            partner_out[i * CHUNK : (i + 1) * CHUNK, :] = product.astype(BF16)
+        else:
+            part[i * CHUNK - HALF : (i + 1) * CHUNK - HALF, :] = product
+
+    pl.semaphore_wait(barrier, len(Z_STEPS) + len(PLANE_STEPS))
     if STOP == 1:
         return finish()
-    to_partner = remote(part.at[0:HALF, :], partner_in, pair_sem.at[0], pair_sem.at[1], dp=y, fsdp=z, tensor=other)
+    to_partner = remote(partner_out, partner_in, pair_sem.at[0], pair_sem.at[1], dp=y, fsdp=z, tensor=other)
     to_partner.start()
     pending.append(to_partner.wait_send)
     to_partner.wait_recv()
-    both = (part[HALF:, :] + partner_in[...]).reshape(CHIPS, OWN, RANK)
+    both = (part[...] + partner_in[...].astype(F32)).reshape(CHIPS, OWN, RANK)
     half[...] = both
     outgoing[...] = both.astype(BF16)
 
@@ -429,8 +433,9 @@
             pltpu.VMEM((LOCAL, LOCAL), BF16),
             pltpu.VMEM((LOCAL, RANK), F32),
             pltpu.VMEM((LOCAL, RANK), BF16),
-            pltpu.VMEM((LOCAL, RANK), F32),
             pltpu.VMEM((HALF, RANK), F32),
+            pltpu.VMEM((HALF, RANK), BF16),
+            pltpu.VMEM((HALF, RANK), BF16),
             pltpu.VMEM((CHIPS, OWN, RANK), F32),
             pltpu.VMEM((CHIPS, OWN, RANK), BF16),
             pltpu.VMEM((CHIPS - 1, OWN, RANK), BF16),

time: 78.1 us -> 76.9 us (0.985)
  Pallas kernels: 77.3 us -> 76.1 us
where the time goes in v4:
time: 76.9 us; the launch traced here: 76.8 us
  Pallas kernels  76.1 us (99%)
    pallas_call x1, Pallas kernels, core(): pl.pallas_call(core_kernel, out_shape=(jax.ShapeDtypeStruct((LOCAL, RANK)...  72.2 us
    pallas_call x1, Pallas kernels, final(): pl.pallas_call(final_kernel, grid=(LOCAL // WIDE,), out_shape=(jax.ShapeD...  3.9 us

profile of v4, /device:TPU:1, one launch (start us, length us, event | category | flops | bytes accessed | tf_op | source)
XLA Modules:
  0.0 76.8 jit_solution(4292330786606910899)
XLA Ops:
  0.6 0.0 copy-start
  0.6 0.0 copy-start.1
  0.7 72.2 %shard_map.58 = (bf16[1024,256]{1,0:T(8,128)(2,1)S(1)}, bf16[256,1024]{1,0:T(8,128)(2,1)S(1)}, f32[256,128]{1,0:T(8,128)S(1)}) custom-call(bf16[1024,1024]{1,0:T(8,128)(2,1)} %bitcast.3, bf16[1024,1024]{1,0:T(8,128)(2,1)} %bitcast.5, f32[1024,256]{1,0:T(8,128)} %f_hbm.1), custom_call_target="tpu_custom_call" | custom-call | tf_op jit(solution)/shard_map/pallas_call | solution.py:421
  72.9 0.0 copy-done
  72.9 0.0 copy-done.1
  72.9 3.9 %shard_map.59 = (f32[1024,1024]{1,0:T(8,128)}, bf16[1024,1024]{1,0:T(8,128)(2,1)}, f32[1024,256]{1,0:T(8,128)}) custom-call(bf16[1024,1024]{1,0:T(8,128)(2,1)S(1)} %bitcast.4, bf16[1024,1024]{1,0:T(8,128)(2,1)S(1)} %bitcast.6, bf16[1024,256]{1,0:T(8,128)(2,1)S(1)} %get-tuple-element.9.o_ref, bf16[256,1024]{1,0:T(8,128)(2,1)S(1)} %get-tuple-element.10.r_ref, ...), custom_call_target="tpu_custom_call" | custom-call | tf_op jit(solution)/shard_map/pallas_call | solution.py:496
Async XLA Ops:
  0.6 72.3 %copy-start = (bf16[1,1024,1024]{2,1,0:T(8,128)(2,1)S(1)}, bf16[1,1024,1024]{2,1,0:T(8,128)(2,1)}, u32[]{:S(2)}) copy-start(bf16[1,1024,1024]{2,1,0:T(8,128)(2,1)} %param.3) | copy-start | bytes 6291460
  0.6 72.3 %copy-start.1 = (bf16[1,1024,1024]{2,1,0:T(8,128)(2,1)S(1)}, bf16[1,1024,1024]{2,1,0:T(8,128)(2,1)}, u32[]{:S(2)}) copy-start(bf16[1,1024,1024]{2,1,0:T(8,128)(2,1)} %param.4) | copy-start | bytes 6291460
